TPU v7x, 256 devices: a whole 4x4x8 slice. The times are simulated.
256 devices in a mesh: seq: 32 (over x, z), head: 8 (over y, core).
Axes of the slice: x: 4, y: 4, z: 8, core: 2. Of those that a mesh axis runs over, the one named last changes fastest.
Arguments:
- tokens: bfloat16 [8192, 3072], P('seq', 'head'), may hold values from -6 to 6
- norm_gain: float32 [3072], replicated, may hold values from 0.1 to 1.9
- w_query: bfloat16 [3072, 3072], P(None, 'head'), may hold values from -0.109375 to 0.109375
- w_key: bfloat16 [3072, 1024], P(None, 'head'), may hold values from -0.3125 to 0.3125
- w_value: bfloat16 [3072, 1024], P(None, 'head'), may hold values from -0.109375 to 0.109375
- w_out: bfloat16 [3072, 3072], P('head'), may hold values from -0.109375 to 0.109375
- keys_cache: bfloat16 [65536, 1024], P('seq', 'head'), may hold values from -120 to 120
- values_cache: bfloat16 [65536, 1024], P('seq', 'head'), may hold values from -6 to 6
- cached_lengths: int32 [4], replicated, may hold values from 0 to 14336, as said below
- rope_offsets: int32 [4], replicated, may hold values from 0 to 8191
Outputs:
- attn_proj: bfloat16 [8192, 3072], P('seq', 'head')
- keys_updated: bfloat16 [65536, 1024], P('seq', 'head')
- values_updated: bfloat16 [65536, 1024], P('seq', 'head')
Inputs may be any that keep to these rules, and one draw needn't show every extreme that they name: `cached_lengths`: in every draw one request has exactly 14336 cached tokens.
All inputs are finite; a program needn't handle non-finite values.
Results may differ from a plain program's by a relative error of at most 0.02.
Values may be sent and summed in bfloat16 or wider, within the bound.
A program may use at most 128 MiB of HBM per device.

v0:
```python
import math
import jax
import jax.numpy as jnp
from jax import lax
from jax.sharding import PartitionSpec as P

HD = 128
rope_base = 500000.0
neg_large = -1e30


def shifted(shard, axis, by):
    devices = lax.axis_size(axis)
    return lax.ppermute(shard, axis, [(i, (i + by) % devices) for i in range(devices)])


def rotate(vectors, positions):
    half_width = vectors.shape[-1] // 2
    frequency = rope_base ** (-jnp.arange(half_width, dtype=jnp.float32) * 2.0 / vectors.shape[-1])
    angles = positions.astype(jnp.float32)[:, None] * frequency[None, :]
    cosine = jnp.cos(angles)[:, None, :]
    sine_part = jnp.sin(angles)[:, None, :]
    first_half = vectors[..., :half_width]
    second_half = vectors[..., half_width:]
    return jnp.concatenate(
        [
            first_half * cosine - second_half * sine_part,
            second_half * cosine + first_half * sine_part,
        ],
        -1,
    )


def shards(
    tokens,
    norm_gain,
    w_query,
    w_key,
    w_value,
    w_out,
    keys_cache,
    values_cache,
    cached_lengths,
    rope_offsets,
):
    gathered = lax.all_gather(tokens, "head", axis=1, tiled=True)
    row_count = gathered.shape[0]
    requests = cached_lengths.shape[0]
    groups = lax.axis_size("seq") // requests
    member = lax.axis_index("seq")
    request = member % requests
    position_in = member // requests
    length = lax.dynamic_index_in_dim(cached_lengths, request, 0, False)
    offset = lax.dynamic_index_in_dim(rope_offsets, request, 0, False)
    widened = gathered.astype(jnp.float32)
    normed = (
        widened * lax.rsqrt(jnp.mean(widened * widened, -1, keepdims=True) + 1e-05) * norm_gain
    ).astype(jnp.bfloat16)
    index_new = position_in * row_count + jnp.arange(row_count, dtype=jnp.int32)
    positions = offset + length + index_new
    kv_heads = w_key.shape[1] // HD
    q_heads = w_query.shape[1] // HD
    repeat = q_heads // kv_heads
    queries = rotate(
        jnp.dot(normed, w_query, preferred_element_type=jnp.float32).reshape(
            row_count, q_heads, HD
        ),
        positions,
    ).astype(jnp.bfloat16)
    new_keys = (
        rotate(
            jnp.dot(normed, w_key, preferred_element_type=jnp.float32).reshape(
                row_count, kv_heads, HD
            ),
            positions,
        )
        .astype(jnp.bfloat16)
        .reshape(row_count, kv_heads * HD)
    )
    new_values = jnp.dot(normed, w_value, preferred_element_type=jnp.float32).astype(jnp.bfloat16)
    grouped = (
        queries.reshape(row_count, kv_heads, repeat, HD)
        .transpose(1, 2, 0, 3)
        .reshape(kv_heads, repeat * row_count, HD)
    )
    slab_rows = keys_cache.shape[0]
    score_scale = 1.0 / math.sqrt(HD)

    def attend(softmax_state, query_group, key_block, value_block, visible):
        running_max, denominator, accumulated = softmax_state
        scores = (
            jnp.einsum(
                "gqd,kgd->gqk",
                query_group,
                key_block.reshape(-1, kv_heads, HD),
                preferred_element_type=jnp.float32,
            )
            * score_scale
        )
        masked = jnp.where(visible, scores, neg_large)
        new_max = jnp.maximum(running_max, jnp.max(masked, -1))
        weights = jnp.where(visible, jnp.exp(masked - new_max[..., None]), 0.0)
        factor = jnp.exp(running_max - new_max)
        denominator = denominator * factor + jnp.sum(weights, -1)
        accumulated = accumulated * factor[..., None] + jnp.einsum(
            "gqk,kgd->gqd",
            weights.astype(jnp.bfloat16),
            value_block.reshape(-1, kv_heads, HD),
            preferred_element_type=jnp.float32,
        )
        return (new_max, denominator, accumulated)

    def attend_pair(
        softmax_state,
        query_anchor,
        query_group,
        slab_keys,
        slab_values,
        slab_source,
        fresh_keys,
        fresh_values,
        fresh_source,
    ):
        query_index = jnp.tile(
            query_anchor * row_count + jnp.arange(row_count, dtype=jnp.int32), repeat
        )
        slots = slab_source * slab_rows + jnp.arange(slab_rows, dtype=jnp.int32)
        old_visible = (slots < length)[None, None, :]
        fresh_index = fresh_source * row_count + jnp.arange(row_count, dtype=jnp.int32)
        fresh_visible = (fresh_index[None, :] <= query_index[:, None])[None]
        softmax_state = attend(softmax_state, query_group, slab_keys, slab_values, old_visible)
        softmax_state = attend(softmax_state, query_group, fresh_keys, fresh_values, fresh_visible)
        return softmax_state

    def write_fresh(out_keys, out_values, fresh_keys, fresh_values, fresh_source):
        fresh_index = fresh_source * row_count + jnp.arange(row_count, dtype=jnp.int32)
        local_slot = length + fresh_index - position_in * slab_rows
        target = jnp.where((local_slot >= 0) & (local_slot < slab_rows), local_slot, slab_rows)
        out_keys = out_keys.at[target].set(fresh_keys, mode="drop")
        out_values = out_values.at[target].set(fresh_values, mode="drop")
        return (out_keys, out_values)

    def absorb(loop_carry, incoming, source):
        softmax_state, out_keys, out_values = loop_carry
        fresh_keys = incoming[0, slab_rows:]
        fresh_values = incoming[1, slab_rows:]
        softmax_state = attend_pair(
            softmax_state,
            position_in,
            grouped,
            incoming[0, :slab_rows],
            incoming[1, :slab_rows],
            source,
            fresh_keys,
            fresh_values,
            source,
        )
        out_keys, out_values = write_fresh(out_keys, out_values, fresh_keys, fresh_values, source)
        return (softmax_state, out_keys, out_values)

    start_state = (
        jnp.full((kv_heads, repeat * row_count), neg_large, jnp.float32),
        jnp.zeros((kv_heads, repeat * row_count), jnp.float32),
        jnp.zeros((kv_heads, repeat * row_count, HD), jnp.float32),
    )
    outgoing = jnp.stack(
        [
            jnp.concatenate([keys_cache, new_keys], 0),
            jnp.concatenate([values_cache, new_values], 0),
        ],
        0,
    )
    loop_carry = absorb((start_state, keys_cache, values_cache), outgoing, position_in)

    def cycle_step(cycle_turn, cycle_carry):
        held_blocks, inner_carry = cycle_carry
        held_blocks = shifted(held_blocks, "seq", requests)
        source = (position_in - cycle_turn) % groups
        return (held_blocks, absorb(inner_carry, held_blocks, source))

    unused, loop_carry = lax.fori_loop(1, groups, cycle_step, (outgoing, loop_carry))
    final_state, keys_updated, values_updated = loop_carry
    running_max, denominator, accumulated = final_state
    attended = (
        (accumulated / denominator[..., None])
        .reshape(kv_heads, repeat, row_count, HD)
        .transpose(2, 0, 1, 3)
        .reshape(row_count, q_heads * HD)
        .astype(jnp.bfloat16)
    )
    partial_value = jnp.dot(attended, w_out, preferred_element_type=jnp.float32)
    summed = lax.psum(partial_value.astype(jnp.bfloat16), "head").astype(jnp.float32)
    share_width = partial_value.shape[1] // lax.axis_size("head")
    projected = lax.dynamic_slice_in_dim(
        summed, lax.axis_index("head") * share_width, share_width, 1
    )
    return (projected.astype(jnp.bfloat16), keys_updated, values_updated)


def solution(mesh):
    return jax.shard_map(
        shards,
        mesh=mesh,
        in_specs=(
            P("seq", "head"),
            P(),
            P(None, "head"),
            P(None, "head"),
            P(None, "head"),
            P("head", None),
            P("seq", "head"),
            P("seq", "head"),
            P(),
            P(),
        ),
        out_specs=(P("seq", "head"), P("seq", "head"), P("seq", "head")),
        check_vma=False,
    )
```

profile of v0, /device:TPU:2, one launch (start us, length us, event | category | flops | bytes accessed | tf_op | source)
XLA Modules:
  0.0 639.8 jit_solution(14705658243390205139)
XLA Ops:
  8.4 2.1 copy.53
  17.2 23.6 %all-gather.2.cloned.1.call-done = bf16[256,3072]{1,0:T(8,128)(2,1)} async-done(((bf16[256,384]{1,0:T(8,128)(2,1)}), bf16[256,3072]{1,0:T(8,128)(2,1)}) %all-gather.2.cloned.1.call-update) | async-done | bytes 1572880 | tf_op jit(solution)/shard_map/all_gather | solution.py:46
  40.8 1.8 fusion.40
  43.2 2.4 convolution_bitcast_fusion.1
  46.1 2.3 convolution_convert_fusion.1
  49.5 3.2 scatter_custom_fusion.2
  53.9 3.2 scatter_custom_fusion.3
  57.1 3.3 fusion.81
  61.2 1.8 copy.20
  63.0 2.1 fusion.37
  66.3 1.6 fusion.39
  71.4 386.1 %while.25 = (s32[]{:T(128)}, bf16[2,2304,128]{2,1,0:T(8,128)(2,1)}, f32[1,768]{1,0:T(1,128)S(1)}, f32[1,768]{1,0:T(1,128)}, f32[1,768,128]{2,1,0:T(8,128)}, /*in...) while((s32[]{:T(128)}, bf16[2,2304,128]{2,1,0:T(8,128)(2,1)}, ...), condition=%wide.region_14.15_spmd, body=%wide.region_7.14_spmd.sunk | while | flops 929181184 | bytes 57951692 | solution.py:181
  71.4 5.7 collective-permute-start
  79.0 41.7 %collective-permute-done = bf16[2,2304,128]{2,1,0:T(8,128)(2,1)S(1)} collective-permute-done((bf16[2,2304,128]{2,1,0:T(8,128)(2,1)}, bf16[2,2304,128]{2,1,0:T(8,128)(2,1)S(1)}, u32[]{:S(2)}, u32[]{:S(2)}) %collective-permute-start) | collective-permute-done | bytes 1179680 | tf_op jit(solution)/shard_map/while/body/eval_jaxpr/ppermute | solution.py:14
  120.7 2.1 fusion.105
  125.4 1.6 fusion.108
  129.5 3.2 scatter_custom_fusion.14
  132.7 3.2 scatter_custom_fusion.15
  135.8 5.2 fusion.109
  141.0 5.1 collective-permute-start
  148.0 23.2 %collective-permute-done = bf16[2,2304,128]{2,1,0:T(8,128)(2,1)S(1)} collective-permute-done((bf16[2,2304,128]{2,1,0:T(8,128)(2,1)}, bf16[2,2304,128]{2,1,0:T(8,128)(2,1)S(1)}, u32[]{:S(2)}, u32[]{:S(2)}) %collective-permute-start) | collective-permute-done | bytes 1179680 | tf_op jit(solution)/shard_map/while/body/eval_jaxpr/ppermute | solution.py:14
  171.2 2.1 fusion.105
  175.9 1.6 fusion.108
  180.0 3.2 scatter_custom_fusion.14
  183.2 3.2 scatter_custom_fusion.15
  186.4 5.2 fusion.109
  191.5 4.2 collective-permute-start
  197.6 27.7 %collective-permute-done = bf16[2,2304,128]{2,1,0:T(8,128)(2,1)S(1)} collective-permute-done((bf16[2,2304,128]{2,1,0:T(8,128)(2,1)}, bf16[2,2304,128]{2,1,0:T(8,128)(2,1)S(1)}, u32[]{:S(2)}, u32[]{:S(2)}) %collective-permute-start) | collective-permute-done | bytes 1179680 | tf_op jit(solution)/shard_map/while/body/eval_jaxpr/ppermute | solution.py:14
  225.3 2.1 fusion.105
  230.1 1.6 fusion.108
  234.1 3.2 scatter_custom_fusion.14
  237.3 3.2 scatter_custom_fusion.15
  240.5 5.2 fusion.109
  245.7 1.6 collective-permute-start
  249.1 29.3 %collective-permute-done = bf16[2,2304,128]{2,1,0:T(8,128)(2,1)S(1)} collective-permute-done((bf16[2,2304,128]{2,1,0:T(8,128)(2,1)}, bf16[2,2304,128]{2,1,0:T(8,128)(2,1)S(1)}, u32[]{:S(2)}, u32[]{:S(2)}) %collective-permute-start) | collective-permute-done | bytes 1179680 | tf_op jit(solution)/shard_map/while/body/eval_jaxpr/ppermute | solution.py:14
  278.4 2.1 fusion.105
  283.2 1.6 fusion.108
  287.2 3.2 scatter_custom_fusion.14
  290.4 3.2 scatter_custom_fusion.15
  293.6 5.2 fusion.109
  298.8 2.8 collective-permute-start
  303.4 27.8 %collective-permute-done = bf16[2,2304,128]{2,1,0:T(8,128)(2,1)S(1)} collective-permute-done((bf16[2,2304,128]{2,1,0:T(8,128)(2,1)}, bf16[2,2304,128]{2,1,0:T(8,128)(2,1)S(1)}, u32[]{:S(2)}, u32[]{:S(2)}) %collective-permute-start) | collective-permute-done | bytes 1179680 | tf_op jit(solution)/shard_map/while/body/eval_jaxpr/ppermute | solution.py:14
  331.2 2.1 fusion.105
  336.0 1.6 fusion.108
  340.0 3.2 scatter_custom_fusion.14
  343.2 3.2 scatter_custom_fusion.15
  346.4 5.2 fusion.109
  351.5 3.2 collective-permute-start
  356.7 27.8 %collective-permute-done = bf16[2,2304,128]{2,1,0:T(8,128)(2,1)S(1)} collective-permute-done((bf16[2,2304,128]{2,1,0:T(8,128)(2,1)}, bf16[2,2304,128]{2,1,0:T(8,128)(2,1)S(1)}, u32[]{:S(2)}, u32[]{:S(2)}) %collective-permute-start) | collective-permute-done | bytes 1179680 | tf_op jit(solution)/shard_map/while/body/eval_jaxpr/ppermute | solution.py:14
  384.5 2.1 fusion.105
  389.3 1.6 fusion.108
  393.3 3.2 scatter_custom_fusion.14
  396.5 3.2 scatter_custom_fusion.15
  399.7 5.2 fusion.109
  404.8 2.6 collective-permute-start
  409.3 27.8 %collective-permute-done = bf16[2,2304,128]{2,1,0:T(8,128)(2,1)S(1)} collective-permute-done((bf16[2,2304,128]{2,1,0:T(8,128)(2,1)}, bf16[2,2304,128]{2,1,0:T(8,128)(2,1)S(1)}, u32[]{:S(2)}, u32[]{:S(2)}) %collective-permute-start) | collective-permute-done | bytes 1179680 | tf_op jit(solution)/shard_map/while/body/eval_jaxpr/ppermute | solution.py:14
  437.1 2.1 fusion.105
  441.9 1.6 fusion.108
  445.9 3.2 scatter_custom_fusion.14
  449.1 3.2 scatter_custom_fusion.15
  452.3 5.2 fusion.109
  459.5 2.2 convolution_convert_fusion
  461.7 169.6 %all-reduce.2.cloned.1.call-done = bf16[256,3072]{1,0:T(8,128)(2,1)} async-done(((bf16[256,3072]{1,0:T(8,128)(2,1)}), bf16[256,3072]{1,0:T(8,128)(2,1)}) %all-reduce.2.cloned.1.call-update) | async-done | bytes 1572880 | tf_op jit(solution)/shard_map/psum | solution.py:192
  631.3 1.6 convert_convert_fusion
  (179 shorter events, 66.0 us)
Async XLA Ops:
  7.2 452.3 %copy-start = (bf16[384,3072]{1,0:T(8,128)(2,1)S(1)}, bf16[384,3072]{1,0:T(8,128)(2,1)}, u32[]{:S(2)}) copy-start(bf16[384,3072]{1,0:T(8,128)(2,1)} %param.17) | copy-start | bytes 7077892
  7.2 36.1 %copy-start.9 = (f32[3072]{0:T(1024)S(1)}, f32[3072]{0:T(1024)}, u32[]{:S(2)}) copy-start(f32[3072]{0:T(1024)} %param.13) | copy-start | bytes 36868
  7.2 33.6 %all-gather.2.cloned.1.call-start = ((), (), s32[]{:S(2)}) async-start(), calls=%async_computation | async-start | bytes 1769472 | tf_op jit(solution)/shard_map/all_gather | solution.py:46
  8.4 37.7 %copy-start.2 = (bf16[2048,128]{1,0:T(8,128)(2,1)}, bf16[2048,128]{1,0:T(8,128)(2,1)S(1)}, u32[]{:S(2)}) copy-start(bf16[2048,128]{1,0:T(8,128)(2,1)S(1)} %copy.52) | copy-start | bytes 1572868
  10.5 620.8 %all-reduce.2.cloned.1.call-start = ((), (), s32[]{:S(2)}) async-start(), calls=%async_computation.1 | async-start | bytes 3145728 | tf_op jit(solution)/shard_map/psum | solution.py:192
  42.6 0.6 copy-start.7
  48.4 8.6 %copy-start.8 = (f32[256]{0:T(256)S(1)}, f32[256]{0:T(256)}, u32[]{:S(2)}) copy-start(f32[256]{0:T(256)} %copy-done.7) | copy-start | bytes 3076
  57.1 3.4 copy-start.3
  57.1 3.4 copy-start.4
  71.4 49.3 %collective-permute-start = (bf16[2,2304,128]{2,1,0:T(8,128)(2,1)}, bf16[2,2304,128]{2,1,0:T(8,128)(2,1)S(1)}, u32[]{:S(2)}, u32[]{:S(2)}) collective-permute-start(bf16[2,2304,128]{2,1,0:T(8,128)(2,1)} %get-tuple-element.428), channel_id=1, source_target_pairs={{0,32},{8,40},{16,48},{24,56},{32,64},{40,72},{48,80},{56,88},{64,... | collective-permute-start | bytes 3538952 | tf_op jit(solution)/shard_map/while/body/eval_jaxpr/ppermute | solution.py:14
  122.8 4.2 copy-start.1
  125.4 1.8 copy-start.5
  127.3 1.2 copy-start.6
  141.0 30.2 %collective-permute-start = (bf16[2,2304,128]{2,1,0:T(8,128)(2,1)}, bf16[2,2304,128]{2,1,0:T(8,128)(2,1)S(1)}, u32[]{:S(2)}, u32[]{:S(2)}) collective-permute-start(bf16[2,2304,128]{2,1,0:T(8,128)(2,1)} %get-tuple-element.428), channel_id=1, source_target_pairs={{0,32},{8,40},{16,48},{24,56},{32,64},{40,72},{48,80},{56,88},{64,... | collective-permute-start | bytes 3538952 | tf_op jit(solution)/shard_map/while/body/eval_jaxpr/ppermute | solution.py:14
  173.3 4.2 copy-start.1
  175.9 1.8 copy-start.5
  177.8 1.2 copy-start.6
  191.5 33.8 %collective-permute-start = (bf16[2,2304,128]{2,1,0:T(8,128)(2,1)}, bf16[2,2304,128]{2,1,0:T(8,128)(2,1)S(1)}, u32[]{:S(2)}, u32[]{:S(2)}) collective-permute-start(bf16[2,2304,128]{2,1,0:T(8,128)(2,1)} %get-tuple-element.428), channel_id=1, source_target_pairs={{0,32},{8,40},{16,48},{24,56},{32,64},{40,72},{48,80},{56,88},{64,... | collective-permute-start | bytes 3538952 | tf_op jit(solution)/shard_map/while/body/eval_jaxpr/ppermute | solution.py:14
  227.4 4.2 copy-start.1
  230.1 1.8 copy-start.5
  231.9 1.2 copy-start.6
  245.7 32.8 %collective-permute-start = (bf16[2,2304,128]{2,1,0:T(8,128)(2,1)}, bf16[2,2304,128]{2,1,0:T(8,128)(2,1)S(1)}, u32[]{:S(2)}, u32[]{:S(2)}) collective-permute-start(bf16[2,2304,128]{2,1,0:T(8,128)(2,1)} %get-tuple-element.428), channel_id=1, source_target_pairs={{0,32},{8,40},{16,48},{24,56},{32,64},{40,72},{48,80},{56,88},{64,... | collective-permute-start | bytes 3538952 | tf_op jit(solution)/shard_map/while/body/eval_jaxpr/ppermute | solution.py:14
  280.5 4.2 copy-start.1
  283.2 1.8 copy-start.5
  285.0 1.2 copy-start.6
  298.8 32.5 %collective-permute-start = (bf16[2,2304,128]{2,1,0:T(8,128)(2,1)}, bf16[2,2304,128]{2,1,0:T(8,128)(2,1)S(1)}, u32[]{:S(2)}, u32[]{:S(2)}) collective-permute-start(bf16[2,2304,128]{2,1,0:T(8,128)(2,1)} %get-tuple-element.428), channel_id=1, source_target_pairs={{0,32},{8,40},{16,48},{24,56},{32,64},{40,72},{48,80},{56,88},{64,... | collective-permute-start | bytes 3538952 | tf_op jit(solution)/shard_map/while/body/eval_jaxpr/ppermute | solution.py:14
  333.3 4.2 copy-start.1
  336.0 1.8 copy-start.5
  337.8 1.2 copy-start.6
  351.5 33.0 %collective-permute-start = (bf16[2,2304,128]{2,1,0:T(8,128)(2,1)}, bf16[2,2304,128]{2,1,0:T(8,128)(2,1)S(1)}, u32[]{:S(2)}, u32[]{:S(2)}) collective-permute-start(bf16[2,2304,128]{2,1,0:T(8,128)(2,1)} %get-tuple-element.428), channel_id=1, source_target_pairs={{0,32},{8,40},{16,48},{24,56},{32,64},{40,72},{48,80},{56,88},{64,... | collective-permute-start | bytes 3538952 | tf_op jit(solution)/shard_map/while/body/eval_jaxpr/ppermute | solution.py:14
  386.6 4.2 copy-start.1
  389.3 1.8 copy-start.5
  391.1 1.2 copy-start.6
  404.8 32.3 %collective-permute-start = (bf16[2,2304,128]{2,1,0:T(8,128)(2,1)}, bf16[2,2304,128]{2,1,0:T(8,128)(2,1)S(1)}, u32[]{:S(2)}, u32[]{:S(2)}) collective-permute-start(bf16[2,2304,128]{2,1,0:T(8,128)(2,1)} %get-tuple-element.428), channel_id=1, source_target_pairs={{0,32},{8,40},{16,48},{24,56},{32,64},{40,72},{48,80},{56,88},{64,... | collective-permute-start | bytes 3538952 | tf_op jit(solution)/shard_map/while/body/eval_jaxpr/ppermute | solution.py:14
  439.2 4.2 copy-start.1
  441.9 1.8 copy-start.5
  443.7 1.2 copy-start.6
Sparse Core Ops, SparseCore 0:
  10.6 30.1 all-gather.1
  461.8 169.4 all-reduce.1
where the time goes:
time: 642 us; the launch traced here: 640 us
  waiting for transfers between devices  399 us (62%)
  matrix products  84.8 us (13%)
  local copies, waits for them, and re-layouts  67 us (10%)
  other arithmetic  48 us (7%)
  starting transfers between devices  25.4 us (4%)
  between operations  15.5 us (2%)
    ppermute x7, waiting for transfers between devices, shifted(): lax.ppermute(shard, axis, [(i, (i + by) % devices) for i in range(devices)])  205 us
    psum x1, waiting for transfers between devices, shards(): lax.psum(partial_value.astype(jnp.bfloat16), 'head').astype(jnp.float32)  170 us
    dot_general x16, matrix products, attend(): jnp.einsum('gqk,kgd->gqd', weights.astype(jnp.bfloat16), value_block.resh...  46.8 us
    dot_general x16, matrix products, attend(): jnp.einsum('gqd,kgd->gqk', query_group, key_block.reshape(-1, kv_heads, H...  27.8 us
    scatter x8, local copies, waits for them, and re-layouts, write_fresh(): out_keys = out_keys.at[target].set(fresh_keys, mode='drop')  25.5 us
    scatter x8, local copies, waits for them, and re-layouts, write_fresh(): out_values = out_values.at[target].set(fresh_values, mode='drop')  25.5 us
    ppermute x7, starting transfers between devices, shifted(): lax.ppermute(shard, axis, [(i, (i + by) % devices) for i in range(devices)])  25.3 us
    all_gather x1, waiting for transfers between devices, shards(): gathered = lax.all_gather(tokens, 'head', axis=1, tiled=True)  23.6 us
  transfers between devices with their start and end apart: 9, of which 9 were waited for; matrix products, arithmetic and copies ran while one was open for 3% of the time, Pallas kernels for 0%

commit v1 on v0

--- a/solution.py
+++ b/solution.py
@@ -43,7 +43,9 @@
     cached_lengths,
     rope_offsets,
 ):
-    gathered = lax.all_gather(tokens, "head", axis=1, tiled=True)
+    gathered = jnp.concatenate(
+        lax.all_to_all(jnp.stack([tokens] * lax.axis_size("head")), "head", 0, 0), axis=1
+    )
     row_count = gathered.shape[0]
     requests = cached_lengths.shape[0]
     groups = lax.axis_size("seq") // requests

time: 642 us -> 673 us (1.048)
  waiting for transfers between devices: 399 us -> 413 us
  local copies, waits for them, and re-layouts: 67 us -> 75.5 us
  starting transfers between devices: 25.4 us -> 33.3 us
    ppermute x7, waiting for transfers between devices: 205 us -> 320 us  [shifted(): lax.ppermute(shard, axis, [(i, (i + by) % devices) for i in range(devices)])]
    psum x1, waiting for transfers between devices: 170 us -> 81.7 us  [shards(): lax.psum(partial_value.astype(jnp.bfloat16), 'head').astype(jnp.float32)]
    all_gather x1 -> x0, waiting for transfers between devices: 23.6 us -> none  [shards(): gathered = lax.all_gather(tokens, 'head', axis=1, tiled=True)]
    all_to_all x0 -> x1, waiting for transfers between devices: none -> 11.4 us  [shards(): lax.all_to_all(jnp.stack([tokens] * lax.axis_size('head')), 'head', 0, 0)]
where the time goes in v1:
time: 673 us; the launch traced here: 671 us
  waiting for transfers between devices  413 us (61%)
  matrix products  80.2 us (12%)
  local copies, waits for them, and re-layouts  75.5 us (11%)
  other arithmetic  52.6 us (8%)
  starting transfers between devices  33.3 us (5%)
  between operations  15.6 us (2%)
    ppermute x7, waiting for transfers between devices, shifted(): lax.ppermute(shard, axis, [(i, (i + by) % devices) for i in range(devices)])  320 us
    psum x1, waiting for transfers between devices, shards(): lax.psum(partial_value.astype(jnp.bfloat16), 'head').astype(jnp.float32)  81.7 us
    dot_general x16, matrix products, attend(): jnp.einsum('gqk,kgd->gqd', weights.astype(jnp.bfloat16), value_block.resh...  46.8 us
    ppermute x7, starting transfers between devices, shifted(): lax.ppermute(shard, axis, [(i, (i + by) % devices) for i in range(devices)])  28.8 us
    dot_general x16, matrix products, attend(): jnp.einsum('gqd,kgd->gqk', query_group, key_block.reshape(-1, kv_heads, H...  27.8 us
    scatter x8, local copies, waits for them, and re-layouts, write_fresh(): out_keys = out_keys.at[target].set(fresh_keys, mode='drop')  25.5 us
    scatter x8, local copies, waits for them, and re-layouts, write_fresh(): out_values = out_values.at[target].set(fresh_values, mode='drop')  25.5 us
    reduce_sum x16, other arithmetic, attend(): denominator = denominator * factor + jnp.sum(weights, -1)  14.2 us
  transfers between devices with their start and end apart: 9, of which 9 were waited for; matrix products, arithmetic and copies ran while one was open for 3% of the time, Pallas kernels for 0%

profile of v1, /device:TPU:2, one launch (start us, length us, event | category | flops | bytes accessed | tf_op | source)
XLA Modules:
  0.0 670.8 jit_solution(15033050906559809790)
XLA Ops:
  8.4 2.1 copy.67
  10.5 2.2 stack.8
  12.7 4.5 all-to-all-start
  18.5 4.3 copy.31
  27.5 11.4 %all-to-all-done = bf16[8,256,384]{2,1,0:T(8,128)(2,1)} async-done(((bf16[8,256,384]{2,1,0:T(8,128)(2,1)}), bf16[8,256,384]{2,1,0:T(8,128)(2,1)}, u32[]{:S(2)}, u32[]{:S(2)}) %all-to-all-start) | async-done | bytes 1572896 | tf_op jit(solution)/shard_map/all_to_all | solution.py:47
  38.9 2.6 copy.29
  41.5 1.9 multiply_reduce_fusion
  43.4 1.9 fusion.41
  47.4 2.2 convolution_convert_fusion.1
  50.7 3.2 scatter_custom_fusion.2
  55.1 3.2 scatter_custom_fusion.3
  58.3 2.0 multiply_convert_fusion
  62.0 1.8 copy.33
  63.8 2.1 fusion.37
  67.1 1.6 fusion.39
  72.2 504.3 %while.25 = (s32[]{:T(128)}, bf16[2,2304,128]{2,1,0:T(8,128)(2,1)}, f32[1,768]{1,0:T(1,128)S(1)}, f32[1,768]{1,0:T(1,128)}, f32[1,768,128]{2,1,0:T(8,128)}, /*in...) while((s32[]{:T(128)}, bf16[2,2304,128]{2,1,0:T(8,128)(2,1)}, ...), condition=%wide.region_14.15_spmd, body=%wide.region_7.14_spmd.sunk | while | flops 929181184 | bytes 57951692 | solution.py:183
  72.2 7.2 %collective-permute-start = (bf16[2,2304,128]{2,1,0:T(8,128)(2,1)}, bf16[2,2304,128]{2,1,0:T(8,128)(2,1)S(1)}, u32[]{:S(2)}, u32[]{:S(2)}) collective-permute-start(bf16[2,2304,128]{2,1,0:T(8,128)(2,1)} %get-tuple-element.428), channel_id=1, source_target_pairs={{0,32},{8,40},{16,48},{24,56},{32,64},{40,72},{48,80},{56,88},{64,... | collective-permute-start | bytes 3538952 | tf_op jit(solution)/shard_map/while/body/eval_jaxpr/ppermute | solution.py:14
  81.2 48.9 %collective-permute-done = bf16[2,2304,128]{2,1,0:T(8,128)(2,1)S(1)} collective-permute-done((bf16[2,2304,128]{2,1,0:T(8,128)(2,1)}, bf16[2,2304,128]{2,1,0:T(8,128)(2,1)S(1)}, u32[]{:S(2)}, u32[]{:S(2)}) %collective-permute-start) | collective-permute-done | bytes 1179680 | tf_op jit(solution)/shard_map/while/body/eval_jaxpr/ppermute | solution.py:14
  130.2 2.1 fusion.104
  134.9 1.6 fusion.107
  138.9 3.2 scatter_custom_fusion.14
  142.1 3.2 scatter_custom_fusion.15
  145.3 5.2 fusion.108
  150.5 6.3 collective-permute-start
  158.7 44.1 %collective-permute-done = bf16[2,2304,128]{2,1,0:T(8,128)(2,1)S(1)} collective-permute-done((bf16[2,2304,128]{2,1,0:T(8,128)(2,1)}, bf16[2,2304,128]{2,1,0:T(8,128)(2,1)S(1)}, u32[]{:S(2)}, u32[]{:S(2)}) %collective-permute-start) | collective-permute-done | bytes 1179680 | tf_op jit(solution)/shard_map/while/body/eval_jaxpr/ppermute | solution.py:14
  202.7 2.1 fusion.104
  207.5 1.6 fusion.107
  211.5 3.2 scatter_custom_fusion.14
  214.7 3.2 scatter_custom_fusion.15
  217.9 5.2 fusion.108
  223.1 5.1 collective-permute-start
  230.0 45.0 %collective-permute-done = bf16[2,2304,128]{2,1,0:T(8,128)(2,1)S(1)} collective-permute-done((bf16[2,2304,128]{2,1,0:T(8,128)(2,1)}, bf16[2,2304,128]{2,1,0:T(8,128)(2,1)S(1)}, u32[]{:S(2)}, u32[]{:S(2)}) %collective-permute-start) | collective-permute-done | bytes 1179680 | tf_op jit(solution)/shard_map/while/body/eval_jaxpr/ppermute | solution.py:14
  275.0 2.1 fusion.104
  279.8 1.6 fusion.107
  283.8 3.2 scatter_custom_fusion.14
  287.0 3.2 scatter_custom_fusion.15
  290.2 5.2 fusion.108
  295.3 3.3 collective-permute-start
  300.5 35.3 %collective-permute-done = bf16[2,2304,128]{2,1,0:T(8,128)(2,1)S(1)} collective-permute-done((bf16[2,2304,128]{2,1,0:T(8,128)(2,1)}, bf16[2,2304,128]{2,1,0:T(8,128)(2,1)S(1)}, u32[]{:S(2)}, u32[]{:S(2)}) %collective-permute-start) | collective-permute-done | bytes 1179680 | tf_op jit(solution)/shard_map/while/body/eval_jaxpr/ppermute | solution.py:14
  335.8 2.1 fusion.104
  340.6 1.6 fusion.107
  344.6 3.2 scatter_custom_fusion.14
  347.8 3.2 scatter_custom_fusion.15
  351.0 5.2 fusion.108
  356.2 6.3 collective-permute-start
  364.4 49.2 %collective-permute-done = bf16[2,2304,128]{2,1,0:T(8,128)(2,1)S(1)} collective-permute-done((bf16[2,2304,128]{2,1,0:T(8,128)(2,1)}, bf16[2,2304,128]{2,1,0:T(8,128)(2,1)S(1)}, u32[]{:S(2)}, u32[]{:S(2)}) %collective-permute-start) | collective-permute-done | bytes 1179680 | tf_op jit(solution)/shard_map/while/body/eval_jaxpr/ppermute | solution.py:14
  413.6 2.1 fusion.104
  418.4 1.6 fusion.107
  422.4 3.2 scatter_custom_fusion.14
  425.6 3.2 scatter_custom_fusion.15
  428.8 5.2 fusion.108
  435.8 53.5 %collective-permute-done = bf16[2,2304,128]{2,1,0:T(8,128)(2,1)S(1)} collective-permute-done((bf16[2,2304,128]{2,1,0:T(8,128)(2,1)}, bf16[2,2304,128]{2,1,0:T(8,128)(2,1)S(1)}, u32[]{:S(2)}, u32[]{:S(2)}) %collective-permute-start) | collective-permute-done | bytes 1179680 | tf_op jit(solution)/shard_map/while/body/eval_jaxpr/ppermute | solution.py:14
  489.3 2.1 fusion.104
  498.1 3.2 scatter_custom_fusion.14
  501.3 3.2 scatter_custom_fusion.15
  504.5 5.2 fusion.108
  512.1 44.1 %collective-permute-done = bf16[2,2304,128]{2,1,0:T(8,128)(2,1)S(1)} collective-permute-done((bf16[2,2304,128]{2,1,0:T(8,128)(2,1)}, bf16[2,2304,128]{2,1,0:T(8,128)(2,1)S(1)}, u32[]{:S(2)}, u32[]{:S(2)}) %collective-permute-start) | collective-permute-done | bytes 1179680 | tf_op jit(solution)/shard_map/while/body/eval_jaxpr/ppermute | solution.py:14
  556.1 2.1 fusion.104
  564.9 3.2 scatter_custom_fusion.14
  568.1 3.2 scatter_custom_fusion.15
  571.3 5.2 fusion.108
  578.5 2.2 convolution_convert_fusion
  580.7 81.7 %all-reduce.2.cloned.1.call-done = bf16[256,3072]{1,0:T(8,128)(2,1)} async-done(((bf16[256,3072]{1,0:T(8,128)(2,1)}), bf16[256,3072]{1,0:T(8,128)(2,1)}) %all-reduce.2.cloned.1.call-update) | async-done | bytes 1572880 | tf_op jit(solution)/shard_map/psum | solution.py:194
  662.4 1.6 convert_convert_fusion
  (198 shorter events, 70.8 us)
Async XLA Ops:
  7.2 571.3 %copy-start = (bf16[384,3072]{1,0:T(8,128)(2,1)S(1)}, bf16[384,3072]{1,0:T(8,128)(2,1)}, u32[]{:S(2)}) copy-start(bf16[384,3072]{1,0:T(8,128)(2,1)} %param.17) | copy-start | bytes 7077892
  8.4 41.2 %copy-start.4 = (bf16[2048,128]{1,0:T(8,128)(2,1)}, bf16[2048,128]{1,0:T(8,128)(2,1)S(1)}, u32[]{:S(2)}) copy-start(bf16[2048,128]{1,0:T(8,128)(2,1)S(1)} %copy.66) | copy-start | bytes 1572868
  8.4 8.9 %copy-start.15 = (s32[4]{0:T(128)S(1)}, s32[4]{0:T(128)}, u32[]{:S(2)}) copy-start(s32[4]{0:T(128)} %param.21) | copy-start | bytes 52
  8.4 9.5 %copy-start.16 = (s32[4]{0:T(128)S(1)}, s32[4]{0:T(128)}, u32[]{:S(2)}) copy-start(s32[4]{0:T(128)} %param.20) | copy-start | bytes 52
  8.4 10.1 %copy-start.9 = (f32[3072]{0:T(1024)S(1)}, f32[3072]{0:T(1024)}, u32[]{:S(2)}) copy-start(f32[3072]{0:T(1024)} %param.13) | copy-start | bytes 36868
  12.7 26.2 %all-to-all-start = ((bf16[8,256,384]{2,1,0:T(8,128)(2,1)}), bf16[8,256,384]{2,1,0:T(8,128)(2,1)}, u32[]{:S(2)}, u32[]{:S(2)}) async-start(bf16[8,256,384]{2,1,0:T(8,128)(2,1)} %stack.8), calls=%async_computation | async-start | bytes 3145728 | tf_op jit(solution)/shard_map/all_to_all | solution.py:47
  17.2 645.2 %all-reduce.2.cloned.1.call-start = ((), (), s32[]{:S(2)}) async-start(), calls=%async_computation.1 | async-start | bytes 3145728 | tf_op jit(solution)/shard_map/psum | solution.py:194
  24.0 21.2 %copy-start.11 = (s32[256]{0:T(256)}, s32[256]{0:T(256)S(1)}, u32[]{:S(2)}) copy-start(s32[256]{0:T(256)S(1)} %get-tuple-element.315) | copy-start | bytes 3076
  41.4 5.0 copy-start.14
  43.4 3.9 copy-start.13
  45.3 1.2 copy-start.2
  58.3 2.1 copy-start.3
  58.3 2.9 copy-start.5
  58.3 2.9 copy-start.6
  60.3 3.4 copy-start.10
  63.8 2.1 copy-start.12
  72.2 58.0 %collective-permute-start = (bf16[2,2304,128]{2,1,0:T(8,128)(2,1)}, bf16[2,2304,128]{2,1,0:T(8,128)(2,1)S(1)}, u32[]{:S(2)}, u32[]{:S(2)}) collective-permute-start(bf16[2,2304,128]{2,1,0:T(8,128)(2,1)} %get-tuple-element.428), channel_id=1, source_target_pairs={{0,32},{8,40},{16,48},{24,56},{32,64},{40,72},{48,80},{56,88},{64,... | collective-permute-start | bytes 3538952 | tf_op jit(solution)/shard_map/while/body/eval_jaxpr/ppermute | solution.py:14
  132.2 4.2 copy-start.1
  134.9 1.8 copy-start.7
  136.7 1.2 copy-start.8
  150.5 52.3 %collective-permute-start = (bf16[2,2304,128]{2,1,0:T(8,128)(2,1)}, bf16[2,2304,128]{2,1,0:T(8,128)(2,1)S(1)}, u32[]{:S(2)}, u32[]{:S(2)}) collective-permute-start(bf16[2,2304,128]{2,1,0:T(8,128)(2,1)} %get-tuple-element.428), channel_id=1, source_target_pairs={{0,32},{8,40},{16,48},{24,56},{32,64},{40,72},{48,80},{56,88},{64,... | collective-permute-start | bytes 3538952 | tf_op jit(solution)/shard_map/while/body/eval_jaxpr/ppermute | solution.py:14
  204.8 4.2 copy-start.1
  207.5 1.8 copy-start.7
  209.3 1.2 copy-start.8
  223.1 52.0 %collective-permute-start = (bf16[2,2304,128]{2,1,0:T(8,128)(2,1)}, bf16[2,2304,128]{2,1,0:T(8,128)(2,1)S(1)}, u32[]{:S(2)}, u32[]{:S(2)}) collective-permute-start(bf16[2,2304,128]{2,1,0:T(8,128)(2,1)} %get-tuple-element.428), channel_id=1, source_target_pairs={{0,32},{8,40},{16,48},{24,56},{32,64},{40,72},{48,80},{56,88},{64,... | collective-permute-start | bytes 3538952 | tf_op jit(solution)/shard_map/while/body/eval_jaxpr/ppermute | solution.py:14
  277.1 4.2 copy-start.1
  279.8 1.8 copy-start.7
  281.6 1.2 copy-start.8
  295.3 40.5 %collective-permute-start = (bf16[2,2304,128]{2,1,0:T(8,128)(2,1)}, bf16[2,2304,128]{2,1,0:T(8,128)(2,1)S(1)}, u32[]{:S(2)}, u32[]{:S(2)}) collective-permute-start(bf16[2,2304,128]{2,1,0:T(8,128)(2,1)} %get-tuple-element.428), channel_id=1, source_target_pairs={{0,32},{8,40},{16,48},{24,56},{32,64},{40,72},{48,80},{56,88},{64,... | collective-permute-start | bytes 3538952 | tf_op jit(solution)/shard_map/while/body/eval_jaxpr/ppermute | solution.py:14
  337.9 4.2 copy-start.1
  340.6 1.8 copy-start.7
  342.4 1.2 copy-start.8
  356.2 57.5 %collective-permute-start = (bf16[2,2304,128]{2,1,0:T(8,128)(2,1)}, bf16[2,2304,128]{2,1,0:T(8,128)(2,1)S(1)}, u32[]{:S(2)}, u32[]{:S(2)}) collective-permute-start(bf16[2,2304,128]{2,1,0:T(8,128)(2,1)} %get-tuple-element.428), channel_id=1, source_target_pairs={{0,32},{8,40},{16,48},{24,56},{32,64},{40,72},{48,80},{56,88},{64,... | collective-permute-start | bytes 3538952 | tf_op jit(solution)/shard_map/while/body/eval_jaxpr/ppermute | solution.py:14
  415.7 4.2 copy-start.1
  418.4 1.8 copy-start.7
  420.2 1.2 copy-start.8
  433.9 55.4 %collective-permute-start = (bf16[2,2304,128]{2,1,0:T(8,128)(2,1)}, bf16[2,2304,128]{2,1,0:T(8,128)(2,1)S(1)}, u32[]{:S(2)}, u32[]{:S(2)}) collective-permute-start(bf16[2,2304,128]{2,1,0:T(8,128)(2,1)} %get-tuple-element.428), channel_id=1, source_target_pairs={{0,32},{8,40},{16,48},{24,56},{32,64},{40,72},{48,80},{56,88},{64,... | collective-permute-start | bytes 3538952 | tf_op jit(solution)/shard_map/while/body/eval_jaxpr/ppermute | solution.py:14
  491.4 4.2 copy-start.1
  494.1 1.8 copy-start.7
  495.9 1.2 copy-start.8
  509.6 46.5 %collective-permute-start = (bf16[2,2304,128]{2,1,0:T(8,128)(2,1)}, bf16[2,2304,128]{2,1,0:T(8,128)(2,1)S(1)}, u32[]{:S(2)}, u32[]{:S(2)}) collective-permute-start(bf16[2,2304,128]{2,1,0:T(8,128)(2,1)} %get-tuple-element.428), channel_id=1, source_target_pairs={{0,32},{8,40},{16,48},{24,56},{32,64},{40,72},{48,80},{56,88},{64,... | collective-permute-start | bytes 3538952 | tf_op jit(solution)/shard_map/while/body/eval_jaxpr/ppermute | solution.py:14
  558.2 4.2 copy-start.1
  560.9 1.8 copy-start.7
  562.7 1.2 copy-start.8
Sparse Core Ops, SparseCore 0:
  580.8 81.5 all-reduce.1
